TPU v7x, 32 devices: a whole 2x2x4 slice. The times are simulated.
32 devices in a mesh: grp: 2 (over x), node: 16 (over z, y, core).
Axes of the slice: x: 2, y: 2, z: 4, core: 2. Of those that a mesh axis runs over, the one named last changes fastest.
Arguments:
- nodes: bfloat16 [128, 2, 1024, 1024], P('grp', None, 'node'), parts along dimension 0, may hold values from -0.34960938 to 0.34960938
- pair_nodes: int32 [16, 2], replicated, may hold values from 0 to 63
- prod_left: int32 [16], replicated, may hold values from 0 to 15, as said below
- prod_right: int32 [16], replicated, may hold values from 0 to 15, each once
- prod_flag: int32 [16], replicated, may hold values from 0 to 1
- prod_diag: int32 [16], replicated, may hold values from 0 to 7, as said below
Outputs:
- diagrams: bfloat16 [16, 2, 1024, 1024], P('grp', None, 'node'), parts along dimension 0
There are 2 independent parts, one for each index of `grp`. A program takes and returns all parts, laid end to end along the dimension named above; an argument that names none is the same for every part. Nothing has to cross between parts.
Inputs may be any that keep to these rules, and one draw needn't show every extreme that they name: `prod_left`: exactly 8 distinct pairs are left operands, each of exactly two products. `prod_diag`: every diagram receives exactly two products.
All inputs are finite; a program needn't handle non-finite values.
Results may differ from a plain program's by a relative error of at most 0.0065.
Values may be sent and summed in bfloat16 or wider, within the bound.
A program may use at most 128 MiB of HBM per device.

v0:
```python
import jax
import jax.numpy as jnp
from jax import lax
from jax.sharding import PartitionSpec as P


def complex_product(left_re, left_im, right_re, right_im):
    real_part = jnp.einsum(
        "lij,ljk->lik", left_re, right_re, preferred_element_type=jnp.float32
    ) - jnp.einsum("lij,ljk->lik", left_im, right_im, preferred_element_type=jnp.float32)
    imag_part = jnp.einsum(
        "lij,ljk->lik", left_re, right_im, preferred_element_type=jnp.float32
    ) + jnp.einsum("lij,ljk->lik", left_im, right_re, preferred_element_type=jnp.float32)
    return jnp.stack([real_part, imag_part], axis=1).astype(jnp.bfloat16)


def adjoint_where(left_re, left_im, my_flags):
    flipped = my_flags[:, None, None] == 1
    return (
        jnp.where(flipped, jnp.swapaxes(left_re, 1, 2), left_re),
        jnp.where(flipped, -jnp.swapaxes(left_im, 1, 2), left_im),
    )


def local(nodes, pair_nodes, prod_left, prod_right, prod_flag, prod_diag):
    position = lax.axis_index("node")
    pairs_all = pair_nodes.shape[0]
    prods_all = prod_left.shape[0]
    diags_all = prods_all // 2
    ordered_nodes = jnp.take(pair_nodes, prod_right, axis=0)
    left_nodes = jnp.take(nodes, ordered_nodes[:, 0], axis=0)
    right_nodes = jnp.take(nodes, ordered_nodes[:, 1], axis=0)
    outgoing = jnp.stack([left_nodes, right_nodes], axis=1)
    assembled = lax.all_to_all(outgoing, "node", split_axis=0, concat_axis=3, tiled=True)
    paired = complex_product(
        assembled[:, 0, 0], assembled[:, 0, 1], assembled[:, 1, 0], assembled[:, 1, 1]
    )
    panels = lax.all_to_all(paired, "node", split_axis=2, concat_axis=0, tiled=True)
    diag_hot = (prod_diag[None, :] == jnp.arange(diags_all, dtype=jnp.int32)[:, None]).astype(
        jnp.int32
    )
    numbers = jnp.arange(pairs_all, dtype=jnp.int32)
    where_pair = jnp.sum(
        (prod_right[None, :] == prod_left[:, None]).astype(jnp.int32) * numbers[None, :], axis=1
    )
    left_sel = jnp.take(panels, where_pair, axis=0)
    left_full = lax.all_to_all(left_sel, "node", split_axis=0, concat_axis=2, tiled=True)
    local_count = left_full.shape[0]
    my_flags = lax.dynamic_slice_in_dim(prod_flag, position * local_count, local_count)
    left_re, left_im = adjoint_where(left_full[:, 0], left_full[:, 1], my_flags)
    results = complex_product(left_re, left_im, paired[:, 0], paired[:, 1])
    result_panels = lax.all_to_all(results, "node", split_axis=2, concat_axis=0, tiled=True)
    rows_all = result_panels.shape[0]
    summed = jnp.dot(
        diag_hot.astype(jnp.bfloat16),
        result_panels.reshape(rows_all, -1),
        preferred_element_type=jnp.float32,
    )
    return summed.reshape(diags_all, 2, result_panels.shape[2], result_panels.shape[3]).astype(
        jnp.bfloat16
    )


def solution(mesh):
    placed = (P("grp", None, "node", None), P(), P(), P(), P(), P())
    return jax.shard_map(
        local, mesh=mesh, in_specs=placed, out_specs=P("grp", None, "node", None), check_vma=False
    )
```

profile of v0, /device:TPU:0, one launch (start us, length us, event | category | flops | bytes accessed | tf_op | source)
XLA Modules:
  0.0 624.5 jit_solution(2190018857934509209)
XLA Ops:
  3.0 8.6 %gather_fusion.2 = bf16[16,2,64,1024]{3,2,1,0:T(8,128)(2,1)} fusion(bf16[64,2,64,1024]{3,2,1,0:T(8,128)(2,1)} %param.8, s32[1024]{0:T(1024)S(1)} %pad_clamp_fusion.2), kind=kCustom, calls=%fused_computation.clone | custom fusion | bytes 8388672 | tf_op jit(solution)/shard_map/jit(_take)/gather | solution.py:31
  11.5 8.5 %gather_fusion.3 = bf16[16,2,64,1024]{3,2,1,0:T(8,128)(2,1)} fusion(bf16[64,2,64,1024]{3,2,1,0:T(8,128)(2,1)} %param.8, s32[1024]{0:T(1024)S(1)} %pad_clamp_fusion.1), kind=kCustom, calls=%fused_computation.1.clone | custom fusion | bytes 8388672 | tf_op jit(solution)/shard_map/jit(_take)/gather | solution.py:32
  25.9 6.2 pad_maximum_fusion
  32.1 8.4 %copy.51 = bf16[16,2,2,64,1024]{4,3,2,1,0:T(8,128)(2,1)} copy(bf16[16,2,2,64,1024]{4,3,2,0,1:T(8,128)(2,1)} %pad_maximum_fusion) | data formatting | bytes 16777216 | tf_op jit(solution)/shard_map/stack | solution.py:33
  40.5 189.5 %all_to_all.69 = bf16[16,2,2,64,1024]{4,3,2,1,0:T(8,128)(2,1)} all-to-all(bf16[16,2,2,64,1024]{4,3,2,1,0:T(8,128)(2,1)} %copy.51), channel_id=1, replica_groups=mesh['grp'=2,'node'=16] {'node'}, dimensions={0} | all-to-all | bytes 16777216 | tf_op jit(solution)/shard_map/all_to_all | solution.py:34
  230.0 8.4 %copy.52 = bf16[16,2,2,64,1024]{4,3,0,2,1:T(8,128)(2,1)} copy(bf16[16,2,2,64,1024]{4,3,2,1,0:T(8,128)(2,1)} %all_to_all.69) | data formatting | bytes 16777216 | tf_op jit(solution)/shard_map/all_to_all | solution.py:34
  238.4 4.7 fusion.15
  251.9 6.4 %copy.53 = bf16[1,2,1024,1024]{3,1,0,2:T(2,128)(2,1)} copy(bf16[1,2,1024,1024]{3,2,1,0:T(8,128)(2,1)S(1)} %pad_maximum_fusion.1) | data formatting | bytes 8388608 | tf_op jit(solution)/shard_map/stack | solution.py:14
  258.3 5.9 all-to-all-start.1
  264.5 77.3 %all-to-all-done.1 = bf16[1,2,1024,1024]{3,1,0,2:T(2,128)(2,1)} async-done(((bf16[1,2,1024,1024]{3,1,0,2:T(2,128)(2,1)}), bf16[1,2,1024,1024]{3,1,0,2:T(2,128)(2,1)}, u32[]{:S(2)}, u32[]{:S(2)}) %all-to-all-start.1) | async-done | bytes 4194336 | tf_op jit(solution)/shard_map/all_to_all | solution.py:38
  341.8 5.5 copy.73
  347.3 5.0 gather_fusion.1
  352.3 4.6 broadcast_select_fusion
  356.9 19.8 %all-to-all-start.2 = ((bf16[16,2,64,1024]{3,2,1,0:T(8,128)(2,1)}), bf16[16,2,64,1024]{3,2,1,0:T(8,128)(2,1)}, u32[]{:S(2)}, u32[]{:S(2)}) async-start(bf16[16,2,64,1024]{3,2,1,0:T(8,128)(2,1)} %broadcast_select_fusion), calls=%async_computation.2 | async-start | bytes 8388608 | tf_op jit(solution)/shard_map/all_to_all | solution.py:47
  378.1 76.2 %all-to-all-done.2 = bf16[16,2,64,1024]{3,2,1,0:T(8,128)(2,1)} async-done(((bf16[16,2,64,1024]{3,2,1,0:T(8,128)(2,1)}), bf16[16,2,64,1024]{3,2,1,0:T(8,128)(2,1)}, u32[]{:S(2)}, u32[]{:S(2)}) %all-to-all-start.2) | async-done | bytes 4194336 | tf_op jit(solution)/shard_map/all_to_all | solution.py:47
  459.5 3.9 copy.58
  463.4 7.3 %fusion.4 = f32[1024,1024]{1,0:T(8,128)} fusion(bf16[1024,1024]{1,0:T(8,128)(2,1)} %copy-done.7, bf16[1,1024,1024]{1,2,0:T(8,128)(2,1)} %copy.58, pred[]{:T(512)} %bitcast.2, bf16[1,2,1024,1024]{3,2,1,0:T(8,128)(2,1)} %bitcast.111), kind=kOutput, calls=%fused_computation.25 | convolution fusion | flops 2149580800 | bytes 10486272 | tf_op jit(solution)/shard_map/lij,ljk->lik/dot_general | solution.py:13
  470.7 4.3 fusion.6
  477.9 6.6 %fusion.3 = bf16[1,1,1024,1024]{3,2,1,0:T(8,128)(2,1)S(1)} fusion(f32[1024,1024]{1,0:T(8,128)} %fusion.4, bf16[1024,1024]{1,0:T(8,128)(2,1)} %copy-done.9, bf16[1,1024,1024]{2,1,0:T(8,128)(2,1)} %copy.57, pred[]{:T(512)} %bitcast.2, bf16[1,2,1024,1024]{3,2,1,0:T(8,128)(2,1)} %bitcast.112), kind=kOutput, calls=%fused_computation.19 | convolution fusion | flops 2150629376 | bytes 12583424 | tf_op jit(solution)/shard_map/lij,ljk->lik/dot_general | solution.py:11
  488.3 6.3 %copy.59 = bf16[1,2,1024,1024]{3,1,0,2:T(2,128)(2,1)} copy(bf16[1,2,1024,1024]{3,2,1,0:T(8,128)(2,1)S(1)} %pad_maximum_fusion.2) | data formatting | bytes 8388608 | tf_op jit(solution)/shard_map/stack | solution.py:14
  494.6 112.0 %all_to_all.70 = bf16[1,2,1024,1024]{3,1,0,2:T(2,128)(2,1)S(1)} all-to-all(bf16[1,2,1024,1024]{3,1,0,2:T(2,128)(2,1)} %copy.59), channel_id=1, replica_groups=mesh['grp'=2,'node'=16] {'node'}, dimensions={2} | all-to-all | bytes 8388608 | tf_op jit(solution)/shard_map/all_to_all | solution.py:52
  606.6 3.3 copy.74
  609.9 4.8 reshape.182
  614.8 4.5 copy.66
  (61 shorter events, 35.1 us)
Async XLA Ops:
  20.0 3.4 copy-start.3
  238.4 4.7 copy-start.4
  247.8 2.4 copy-start.9
  250.2 1.3 copy-start.7
  258.3 5.9 copy-start.12
  258.3 5.9 copy-start.13
  258.3 83.5 %all-to-all-start.1 = ((bf16[1,2,1024,1024]{3,1,0,2:T(2,128)(2,1)}), bf16[1,2,1024,1024]{3,1,0,2:T(2,128)(2,1)}, u32[]{:S(2)}, u32[]{:S(2)}) async-start(bf16[1,2,1024,1024]{3,1,0,2:T(2,128)(2,1)} %copy.53), calls=%async_computation.1 | async-start | bytes 8388608 | tf_op jit(solution)/shard_map/all_to_all | solution.py:38
  356.9 19.8 %copy-start.14 = (s32[16]{0:T(128)S(1)}, s32[16]{0:T(128)}, u32[]{:S(2)}) copy-start(s32[16]{0:T(128)} %param.12) | copy-start | bytes 196
  356.9 97.4 %all-to-all-start.2 = ((bf16[16,2,64,1024]{3,2,1,0:T(8,128)(2,1)}), bf16[16,2,64,1024]{3,2,1,0:T(8,128)(2,1)}, u32[]{:S(2)}, u32[]{:S(2)}) async-start(bf16[16,2,64,1024]{3,2,1,0:T(8,128)(2,1)} %broadcast_select_fusion), calls=%async_computation.2 | async-start | bytes 8388608 | tf_op jit(solution)/shard_map/all_to_all | solution.py:47
  456.9 2.6 copy-start
  463.4 7.3 %copy-start.1 = (bf16[1,2,16,64,1024]{4,3,2,1,0:T(8,128)(2,1)S(1)}, bf16[1,2,16,64,1024]{4,3,2,1,0:T(8,128)(2,1)}, u32[]{:S(2)}) copy-start(bf16[1,2,16,64,1024]{4,3,2,1,0:T(8,128)(2,1)} %copy-done) | copy-start | bytes 12582916
  463.4 7.3 %copy-start.6 = (bf16[1,1024,1024]{1,2,0:T(8,128)(2,1)S(1)}, bf16[1,1024,1024]{1,2,0:T(8,128)(2,1)}, u32[]{:S(2)}) copy-start(bf16[1,1024,1024]{1,2,0:T(8,128)(2,1)} %copy.58) | copy-start | bytes 6291460
  463.4 7.3 %copy-start.10 = (bf16[1024,1024]{1,0:T(8,128)(2,1)S(1)}, bf16[1024,1024]{1,0:T(8,128)(2,1)}, u32[]{:S(2)}) copy-start(bf16[1024,1024]{1,0:T(8,128)(2,1)} %copy-done.9) | copy-start | bytes 6291460
  477.8 6.6 %copy-start.2 = (bf16[1,2,16,64,1024]{4,3,2,1,0:T(8,128)(2,1)S(1)}, bf16[1,2,16,64,1024]{4,3,2,1,0:T(8,128)(2,1)}, u32[]{:S(2)}) copy-start(bf16[1,2,16,64,1024]{4,3,2,1,0:T(8,128)(2,1)} %copy-done) | copy-start | bytes 12582916
  477.8 6.6 %copy-start.5 = (bf16[1,1024,1024]{2,1,0:T(8,128)(2,1)S(1)}, bf16[1,1024,1024]{2,1,0:T(8,128)(2,1)}, u32[]{:S(2)}) copy-start(bf16[1,1024,1024]{2,1,0:T(8,128)(2,1)} %copy.57) | copy-start | bytes 6291460
  477.8 6.6 %copy-start.8 = (bf16[1024,1024]{1,0:T(8,128)(2,1)S(1)}, bf16[1024,1024]{1,0:T(8,128)(2,1)}, u32[]{:S(2)}) copy-start(bf16[1024,1024]{1,0:T(8,128)(2,1)} %copy-done.7) | copy-start | bytes 6291460
  477.9 7.7 %copy-start.15 = (f32[1024,1024]{1,0:T(8,128)S(1)}, f32[1024,1024]{1,0:T(8,128)}, u32[]{:S(2)}) copy-start(f32[1024,1024]{1,0:T(8,128)} %fusion.6) | copy-start | bytes 12582916
  614.8 4.5 copy-start.11
where the time goes:
time: 629 us; the launch traced here: 624 us
  blocking collectives  301 us (48%)
  waiting for transfers between devices  153 us (24%)
  local copies, waits for them, and re-layouts  89.5 us (14%)
  matrix products  34.6 us (6%)
  starting transfers between devices  25.7 us (4%)
  other arithmetic  18.4 us (3%)
    all_to_all x1, blocking collectives, local(): lax.all_to_all(outgoing, 'node', split_axis=0, concat_axis=3, tiled=True)  189 us
    all_to_all x1, blocking collectives, local(): lax.all_to_all(results, 'node', split_axis=2, concat_axis=0, tiled=True)  112 us
    all_to_all x1, waiting for transfers between devices, local(): lax.all_to_all(paired, 'node', split_axis=2, concat_axis=0, tiled=True)  77.3 us
    all_to_all x1, waiting for transfers between devices, local(): lax.all_to_all(left_sel, 'node', split_axis=0, concat_axis=2, tiled=True)  76.2 us
    all_to_all x1, starting transfers between devices, local(): lax.all_to_all(left_sel, 'node', split_axis=0, concat_axis=2, tiled=True)  19.8 us
    another operation x2, local copies, waits for them, and re-layouts, complex_product(): return jnp.stack([real_part, imag_part], axis=1).astype(jnp.bfloat16)  12.7 us
  transfers between devices with their start and end apart: 2, of which 2 were waited for; matrix products, arithmetic and copies ran while one was open for 0% of the time, Pallas kernels for 0%

commit v1 on v0

v1 whole, which is shorter than its diff:
```python
import functools

import jax
import jax.numpy as jnp
from jax import lax
from jax.experimental import pallas as pl
from jax.experimental.pallas import tpu as pltpu
from jax.sharding import PartitionSpec as P

TILE = 256


def gather_kernel(left_ids, a_ids, b_ids, left_in, a_in, b_in, left_out, a_out, b_out):
    del left_ids, a_ids, b_ids
    left_out[...] = left_in[...]
    a_out[...] = a_in[...]
    chunks = b_out.shape[0]
    width = b_out.shape[-1]
    for c in range(chunks):
        b_out[c] = b_in[:, :, :, c * width : (c + 1) * width]


def gather(nodes, left_ids, a_ids, b_ids, chunks):
    count = a_ids.shape[0]
    _, parts, rows, order = nodes.shape
    width = order // chunks
    block = (1, parts, rows, order)
    whole = jax.ShapeDtypeStruct((count, parts, rows, order), nodes.dtype)
    cut = jax.ShapeDtypeStruct((chunks, count, parts, rows, width), nodes.dtype)
    return pl.pallas_call(
        gather_kernel,
        out_shape=(whole, whole, cut),
        grid_spec=pltpu.PrefetchScalarGridSpec(
            num_scalar_prefetch=3,
            grid=(count,),
            in_specs=[
                pl.BlockSpec(block, lambda i, l, a, b: (l[i], 0, 0, 0)),
                pl.BlockSpec(block, lambda i, l, a, b: (a[i], 0, 0, 0)),
                pl.BlockSpec(block, lambda i, l, a, b: (b[i], 0, 0, 0)),
            ],
            out_specs=[
                pl.BlockSpec(block, lambda i, l, a, b: (i, 0, 0, 0)),
                pl.BlockSpec(block, lambda i, l, a, b: (i, 0, 0, 0)),
                pl.BlockSpec((chunks, 1, parts, rows, width), lambda i, l, a, b: (0, i, 0, 0, 0)),
            ],
        ),
        compiler_params=pltpu.CompilerParams(vmem_limit_bytes=16 * 2**20),
    )(left_ids, a_ids, b_ids, nodes, nodes, nodes)


def tile_product(left_re, left_im, right_re, right_im):
    dot = functools.partial(jnp.dot, preferred_element_type=jnp.float32)
    real_part = dot(left_re, right_re) - dot(left_im, right_im)
    imag_part = dot(left_re, right_im) + dot(left_im, right_re)
    return real_part.astype(jnp.bfloat16), imag_part.astype(jnp.bfloat16)


def exchange_kernel(
    n,
    flags,
    slots,
    left_send,
    a_send,
    b_send,
    out,
    lefts,
    a_full,
    b_full,
    left_plain,
    left_used,
    right_pair,
    result,
    panels,
    left_sem,
    a_sem,
    b_sem,
    swap_sem,
    result_sem,
    left_out_sem,
    a_out_sem,
    b_out_sem,
    swap_out_sem,
    result_out_sem,
):
    me = lax.axis_index("node")
    parity = lax.rem(me, 2)
    partner = me + 1 - 2 * parity
    chunks = b_full.shape[0]
    order = a_full.shape[1]
    rows = left_send.shape[2]
    tiles = order // TILE
    my_rows = pl.ds(pl.multiple_of(me * rows, rows), rows)

    def target(t):
        half = lax.div(t + 1, 2)
        return lax.rem(me + n // 2 + (2 * lax.rem(t, 2) - 1) * half, n)

    barrier = pltpu.get_barrier_semaphore()

    @pl.loop(0, n - 1)
    def _(t):
        pl.semaphore_signal(
            barrier,
            inc=1,
            device_id={"node": target(t)},
            device_id_type=pl.DeviceIdType.MESH,
        )

    pl.semaphore_wait(barrier, n - 1)

    def push(src, dst, send_sem, recv_sem, to):
        pltpu.make_async_remote_copy(
            src_ref=src,
            dst_ref=dst,
            send_sem=send_sem,
            recv_sem=recv_sem,
            device_id={"node": to},
            device_id_type=pl.DeviceIdType.MESH,
        ).start()

    def landed(ref, sem):
        pltpu.make_async_copy(ref, ref, sem).wait()

    @pl.loop(0, n - 1)
    def _(t):
        to = target(t)
        push(left_send.at[to], lefts.at[lax.rem(to, 2), :, my_rows], left_out_sem, left_sem, to)

    pltpu.make_async_copy(left_send.at[me], lefts.at[parity, :, my_rows], left_sem).start()

    @pl.loop(0, n - 1)
    def _(t):
        to = target(t)
        push(a_send.at[to], a_full.at[:, my_rows], a_out_sem, a_sem, to)

    pltpu.make_async_copy(a_send.at[me], a_full.at[:, my_rows], a_sem).start()

    @pl.loop(0, chunks)
    def _(c):
        @pl.loop(0, n - 1)
        def _(t):
            to = target(t)
            push(b_send.at[c, to], b_full.at[c, :, my_rows], b_out_sem.at[c], b_sem.at[c], to)

        pltpu.make_async_copy(b_send.at[c, me], b_full.at[c, :, my_rows], b_sem.at[c]).start()

    landed(lefts.at[parity], left_sem)
    push(lefts.at[parity], lefts.at[parity], swap_out_sem, swap_sem, partner)
    landed(lefts.at[1 - parity], swap_sem)

    def block(i):
        return pl.ds(pl.multiple_of(i * TILE, TILE), TILE)

    @pl.loop(0, tiles * tiles)
    def _(t):
        down, across = block(lax.div(t, tiles)), block(lax.rem(t, tiles))
        real_part, imag_part = tile_product(
            lefts[0, 0, down, :], lefts[0, 1, down, :], lefts[1, 0, :, across], lefts[1, 1, :, across]
        )
        left_plain[0, down, across] = real_part
        left_plain[1, down, across] = imag_part

    flipped = flags[me] == 1

    @pl.loop(0, tiles * tiles)
    def _(t):
        down, across = block(lax.div(t, tiles)), block(lax.rem(t, tiles))
        left_used[0, down, across] = jnp.where(
            flipped, left_plain[0, across, down].T, left_plain[0, down, across]
        )
        left_used[1, down, across] = jnp.where(
            flipped, -left_plain[1, across, down].T, left_plain[1, down, across]
        )

    landed(a_full, a_sem)

    for c in range(chunks):
        landed(b_full.at[c], b_sem.at[c])

        @pl.loop(0, tiles)
        def _(i):
            down = block(i)
            real_part, imag_part = tile_product(
                a_full[0, down, :], a_full[1, down, :], b_full[c, 0], b_full[c, 1]
            )
            right_pair[0, down, :] = real_part
            right_pair[1, down, :] = imag_part

        @pl.loop(0, tiles)
        def _(i):
            down = block(i)
            real_part, imag_part = tile_product(
                left_used[0, down, :], left_used[1, down, :], right_pair[0], right_pair[1]
            )
            result[c, 0, down, :] = real_part
            result[c, 1, down, :] = imag_part

        @pl.loop(0, n - 1)
        def _(t):
            to = target(t)
            to_rows = pl.ds(pl.multiple_of(to * rows, rows), rows)
            push(
                result.at[c, :, to_rows],
                panels[c].at[me],
                result_out_sem.at[c],
                result_sem.at[c],
                to,
            )

        pltpu.make_async_copy(
            result.at[c, :, my_rows], panels[c].at[me], result_sem.at[c]
        ).start()

    width = b_full.shape[-1]
    for c in range(chunks):
        landed(panels[c], result_sem.at[c])

        @pl.loop(0, out.shape[0])
        def _(d):
            first = panels[c][slots[d, 0]].astype(jnp.float32)
            second = panels[c][slots[d, 1]].astype(jnp.float32)
            out[d, :, :, c * width : (c + 1) * width] = (first + second).astype(out.dtype)

    others = pl.ds(0, n - 1)
    landed(left_send.at[others], left_out_sem)
    landed(a_send.at[others], a_out_sem)
    landed(lefts.at[parity], swap_out_sem)
    for c in range(chunks):
        landed(b_send.at[c, others], b_out_sem.at[c])
        landed(panels[c].at[others], result_out_sem.at[c])


def local(nodes, pair_nodes, prod_left, prod_right, prod_flag, prod_diag, *, n):
    _, parts, rows, order = nodes.shape
    count = prod_left.shape[0]
    assert count == n and rows * n == order
    diags = count // 2
    chunks = order // TILE
    numbers = jnp.arange(count, dtype=jnp.int32)
    ahead = (prod_left[None, :] < prod_left[:, None]) | (
        (prod_left[None, :] == prod_left[:, None]) & (numbers[None, :] < numbers[:, None])
    )
    rank = jnp.sum(ahead.astype(jnp.int32), axis=1)
    here = rank[None, :] == numbers[:, None]

    def ordered(values):
        return jnp.sum(jnp.where(here, values[None, :], 0), axis=1)

    left_of, right_of = ordered(prod_left), ordered(prod_right)
    flag_of, diag_of = ordered(prod_flag), ordered(prod_diag)

    def node_of(pairs, side):
        hot = pairs[:, None] == jnp.arange(pair_nodes.shape[0], dtype=jnp.int32)[None, :]
        return jnp.sum(jnp.where(hot, side, 0), axis=1)

    side = jnp.where(numbers[:, None] % 2 == 0, pair_nodes[None, :, 0], pair_nodes[None, :, 1])
    left_ids = node_of(left_of, side)
    a_ids = node_of(right_of, pair_nodes[None, :, 0])
    b_ids = node_of(right_of, pair_nodes[None, :, 1])
    mine = diag_of[None, :] == jnp.arange(diags, dtype=jnp.int32)[:, None]
    first = jnp.min(jnp.where(mine, numbers[None, :], count), axis=1)
    last = jnp.max(jnp.where(mine, numbers[None, :], -1), axis=1)
    slots = jnp.stack([first, last], axis=1)

    left_send, a_send, b_send = gather(nodes, left_ids, a_ids, b_ids, chunks)
    width = order // chunks
    kind = nodes.dtype
    dma = pltpu.SemaphoreType.DMA
    smem = pl.BlockSpec(memory_space=pltpu.SMEM)
    anywhere = pl.BlockSpec(memory_space=pl.ANY)
    return pl.pallas_call(
        functools.partial(exchange_kernel, n),
        out_shape=jax.ShapeDtypeStruct((diags, parts, rows, order), kind),
        in_specs=[smem, smem, anywhere, anywhere, anywhere],
        out_specs=pl.BlockSpec(memory_space=pltpu.VMEM),
        scratch_shapes=[
            pltpu.VMEM((2, parts, order, order), kind),
            pltpu.VMEM((parts, order, order), kind),
            pltpu.VMEM((chunks, parts, order, width), kind),
            pltpu.VMEM((parts, order, order), kind),
            pltpu.VMEM((parts, order, order), kind),
            pltpu.VMEM((parts, order, width), kind),
            pltpu.VMEM((chunks, parts, order, width), kind),
            [pltpu.VMEM((count, parts, rows, width), kind)] * chunks,
            dma,
            dma,
            dma((chunks,)),
            dma,
            dma((chunks,)),
            dma,
            dma,
            dma((chunks,)),
            dma,
            dma((chunks,)),
        ],
        compiler_params=pltpu.CompilerParams(
            collective_id=0, has_side_effects=True, vmem_limit_bytes=56 * 2**20
        ),
    )(flag_of, slots, left_send, a_send, b_send)


def solution(mesh):
    placed = (P("grp", None, "node", None), P(), P(), P(), P(), P())
    return jax.shard_map(
        functools.partial(local, n=mesh.shape["node"]),
        mesh=mesh,
        in_specs=placed,
        out_specs=P("grp", None, "node", None),
        check_vma=False,
    )
```

time: 629 us -> 390 us (0.62)
  Pallas kernels: 0 us -> 371 us
  blocking collectives: 301 us -> 0 us
  waiting for transfers between devices: 153 us -> 0 us
  local copies, waits for them, and re-layouts: 89.5 us -> 16.2 us
  matrix products: 34.6 us -> 0 us
  starting transfers between devices: 25.7 us -> 0 us
  other arithmetic: 18.4 us -> 2.69 us
    pallas_call x0 -> x2, Pallas kernels: none -> 371 us  [the longest x1 369 us: local(): pl.pallas_call(functools.partial(exchange_kernel, n), out_shape=jax.Shape...]
    all_to_all x2 -> x0, blocking collectives: 301 us -> none  [the longest x1 189 us: local(): lax.all_to_all(outgoing, 'node', split_axis=0, concat_axis=3, tiled=True)]
    all_to_all x2 -> x0, waiting for transfers between devices: 153 us -> none  [the longest x1 77.3 us: local(): lax.all_to_all(paired, 'node', split_axis=2, concat_axis=0, tiled=True)]
    dot_general x9 -> x0, matrix products: 34.6 us -> none  [the longest x2 11.2 us: complex_product(): jnp.einsum('lij,ljk->lik', left_re, right_im, preferred_element_type=jnp....]
    all_to_all x2 -> x0, starting transfers between devices: 25.7 us -> none  [the longest x1 19.8 us: local(): lax.all_to_all(left_sel, 'node', split_axis=0, concat_axis=2, tiled=True)]
    gather x4 -> x0, local copies, waits for them, and re-layouts: 22.6 us -> none  [the longest x1 8.55 us: local(): left_nodes = jnp.take(nodes, ordered_nodes[:, 0], axis=0)]
    another operation x3 -> x1, local copies, waits for them, and re-layouts: 21.1 us -> 0.68 us  [local(): slots = jnp.stack([first, last], axis=1)]
    all_to_all x4 -> x0, local copies, waits for them, and re-layouts: 19.9 us -> none  [the longest x1 8.42 us: local(): lax.all_to_all(outgoing, 'node', split_axis=0, concat_axis=3, tiled=True)]
  transfers between devices with their start and end apart: 2 -> 0, of which waited for: 2 -> 0; matrix products, arithmetic and copies ran while one was open for 0% -> 0% of each run, Pallas kernels for 0% -> 0%
where the time goes in v1:
time: 390 us
  Pallas kernels  371 us (95%)
  local copies, waits for them, and re-layouts  16.2 us (4%)
    pallas_call x1, Pallas kernels, local(): pl.pallas_call(functools.partial(exchange_kernel, n), out_shape=jax.Shape...  369 us
    unnamed x9, local copies, waits for them, and re-layouts  14.8 us

profile of v1, /device:TPU:0, one launch (start us, length us, event | category | flops | bytes accessed | tf_op | source)
XLA Modules:
  0.0 389.6 jit_solution(11044106078096791198)
XLA Ops:
  0.0 0.9 convert_reduce_fusion
  0.9 0.8 slice_bitcast_fusion.1
  1.7 1.4 select_reduce_fusion.2
  3.1 0.2 select_reduce_fusion
  3.3 0.2 select_reduce_fusion.8
  3.5 0.7 copy.10.slots
  4.1 0.0 copy-start
  4.1 5.8 %copy-done = bf16[64,2,64,1024]{3,2,1,0:T(8,128)(2,1)S(1)} copy-done((bf16[64,2,64,1024]{3,2,1,0:T(8,128)(2,1)S(1)}, bf16[64,2,64,1024]{3,2,1,0:T(8,128)(2,1)}, u32[]{:S(2)}) %copy-start) | copy-done | bytes 16777240
  9.9 1.9 shard_map.64
  11.8 0.0 copy-start.1
  11.8 1.9 copy-done.1
  13.8 0.0 copy-start.2
  13.8 2.0 copy-done.2
  15.7 0.0 copy-start.3
  15.7 2.0 copy-done.3
  17.7 368.8 %shard_map.65 = bf16[8,2,64,1024]{3,2,1,0:T(8,128)(2,1)} custom-call(s32[16]{0:T(128)} %get-tuple-element.17.flags, s32[8,2]{1,0:T(8,128)} %copy.10.slots, bf16[16,2,64,1024]{3,2,1,0:T(8,128)(2,1)} %copy-done.1, bf16[16,2,64,1024]{3,2,1,0:T(8,128)(2,1)} %copy-done.2, bf16[4,16,2,64,256]{4,3,2,1,0:T(8,128)(2,1)} %copy-done.3), custom_call_target="tpu_custom_call" | custom-call | tf_op jit(solution)/shard_map/pallas_call | solution.py:271
  386.5 3.1 copy.12
  (2 shorter events, 0.0 us)
Async XLA Ops:
  4.1 5.8 %copy-start = (bf16[64,2,64,1024]{3,2,1,0:T(8,128)(2,1)S(1)}, bf16[64,2,64,1024]{3,2,1,0:T(8,128)(2,1)}, u32[]{:S(2)}) copy-start(bf16[64,2,64,1024]{3,2,1,0:T(8,128)(2,1)} %b_in.1) | copy-start | bytes 50331652
  11.8 1.9 copy-start.1
  13.8 2.0 copy-start.2
  15.7 2.0 copy-start.3

commit v2 on v1

--- a/solution.py
+++ b/solution.py
@@ -10,42 +10,160 @@
 TILE = 256
 
 
-def gather_kernel(left_ids, a_ids, b_ids, left_in, a_in, b_in, left_out, a_out, b_out):
-    del left_ids, a_ids, b_ids
-    left_out[...] = left_in[...]
-    a_out[...] = a_in[...]
+def plan_and_gather_kernel(
+    pair_nodes,
+    prod_left,
+    prod_right,
+    prod_flag,
+    prod_diag,
+    nodes,
+    flags,
+    merges,
+    finals,
+    left_out,
+    a_out,
+    b_out,
+    seen_left,
+    seen_diag,
+    mate_left,
+    mate_diag,
+    done,
+    slot_of,
+    order,
+    left_sem,
+    a_sem,
+    b_sem,
+):
+    count = prod_left.shape[0]
+    diags = count // 2
+    half = count // 2
+    slots = half // 2 + 1
     chunks = b_out.shape[0]
     width = b_out.shape[-1]
-    for c in range(chunks):
-        b_out[c] = b_in[:, :, :, c * width : (c + 1) * width]
-
-
-def gather(nodes, left_ids, a_ids, b_ids, chunks):
-    count = a_ids.shape[0]
+
+    @pl.loop(0, pair_nodes.shape[0])
+    def _(p):
+        seen_left[p] = -1
+
+    @pl.loop(0, diags)
+    def _(d):
+        seen_diag[d] = -1
+        slot_of[d] = -1
+        slot_of[diags + d] = -1
+
+    @pl.loop(0, count)
+    def _(k):
+        done[k] = 0
+        for group, seen, mate in (
+            (prod_left[k], seen_left, mate_left),
+            (prod_diag[k], seen_diag, mate_diag),
+        ):
+            earlier = seen[group]
+            found = earlier >= 0
+            mate[k] = earlier
+            back = jnp.where(found, earlier, k)
+            mate[back] = jnp.where(found, k, mate[back])
+            seen[group] = k
+
+    def place(g, now):
+        other = mate_left[now]
+        done[now] = 1
+        done[other] = 1
+        order[2 * g] = now
+        order[2 * g + 1] = other
+        for at, k in ((2 * g, now), (2 * g + 1, other)):
+            flags[at] = prod_flag[k]
+            left_id = pair_nodes[prod_left[k], at - 2 * g]
+            right = prod_right[k]
+            pltpu.make_async_copy(nodes.at[left_id], left_out.at[at], left_sem).start()
+            pltpu.make_async_copy(nodes.at[pair_nodes[right, 0]], a_out.at[at], a_sem).start()
+            for c in range(chunks):
+                pltpu.make_async_copy(
+                    nodes.at[pair_nodes[right, 1], :, :, pl.ds(c * width, width)],
+                    b_out.at[c, at],
+                    b_sem,
+                ).start()
+        free = lax.fori_loop(
+            0,
+            count,
+            lambda k, best: jnp.where(done[count - 1 - k] == 0, count - 1 - k, best),
+            jnp.int32(0),
+        )
+        follow = mate_diag[other]
+        return jnp.where(done[follow] == 0, follow, free)
+
+    lax.fori_loop(0, count // 2, place, jnp.int32(0))
+
+    for h in range(2):
+        base = h * slots
+
+        @pl.loop(0, slots)
+        def _(t):
+            merges[2 * (base + t)] = half
+            merges[2 * (base + t) + 1] = half
+
+        def take(i, used):
+            diag = prod_diag[order[h * half + i]]
+            slot = slot_of[h * diags + diag]
+            new = slot < 0
+            slot = jnp.where(new, used, slot)
+            slot_of[h * diags + diag] = slot
+            at = 2 * (base + slot)
+            merges[at] = jnp.where(new, i, merges[at])
+            merges[at + 1] = jnp.where(new, half, i)
+            return used + new.astype(jnp.int32)
+
+        lax.fori_loop(0, half, take, jnp.int32(0))
+
+    for h in range(2):
+
+        @pl.loop(0, diags)
+        def _(d):
+            near = slot_of[h * diags + d]
+            far = half + slot_of[(1 - h) * diags + d]
+            here = near >= 0
+            at = 2 * (h * slots + jnp.maximum(near, 0))
+            both = here & (merges[at + 1] < half)
+            finals[2 * (h * diags + d)] = jnp.where(here, merges[at], far)
+            finals[2 * (h * diags + d) + 1] = jnp.where(
+                both, merges[at + 1], jnp.where(here, far, half + slots)
+            )
+
+    pltpu.make_async_copy(left_out, left_out, left_sem).wait()
+    pltpu.make_async_copy(a_out, a_out, a_sem).wait()
+    pltpu.make_async_copy(b_out, b_out, b_sem).wait()
+
+
+def plan_and_gather(nodes, pair_nodes, prod_left, prod_right, prod_flag, prod_diag, chunks):
+    count = prod_left.shape[0]
     _, parts, rows, order = nodes.shape
-    width = order // chunks
-    block = (1, parts, rows, order)
+    half = count // 2
+    slots = half // 2 + 1
     whole = jax.ShapeDtypeStruct((count, parts, rows, order), nodes.dtype)
-    cut = jax.ShapeDtypeStruct((chunks, count, parts, rows, width), nodes.dtype)
+    cut = jax.ShapeDtypeStruct((chunks, count, parts, rows, order // chunks), nodes.dtype)
+    table = lambda size: jax.ShapeDtypeStruct((size,), jnp.int32)
+    smem = pl.BlockSpec(memory_space=pltpu.SMEM)
+    anywhere = pl.BlockSpec(memory_space=pl.ANY)
+    scratch = lambda size: pltpu.SMEM((size,), jnp.int32)
     return pl.pallas_call(
-        gather_kernel,
-        out_shape=(whole, whole, cut),
-        grid_spec=pltpu.PrefetchScalarGridSpec(
-            num_scalar_prefetch=3,
-            grid=(count,),
-            in_specs=[
-                pl.BlockSpec(block, lambda i, l, a, b: (l[i], 0, 0, 0)),
-                pl.BlockSpec(block, lambda i, l, a, b: (a[i], 0, 0, 0)),
-                pl.BlockSpec(block, lambda i, l, a, b: (b[i], 0, 0, 0)),
-            ],
-            out_specs=[
-                pl.BlockSpec(block, lambda i, l, a, b: (i, 0, 0, 0)),
-                pl.BlockSpec(block, lambda i, l, a, b: (i, 0, 0, 0)),
-                pl.BlockSpec((chunks, 1, parts, rows, width), lambda i, l, a, b: (0, i, 0, 0, 0)),
-            ],
-        ),
-        compiler_params=pltpu.CompilerParams(vmem_limit_bytes=16 * 2**20),
-    )(left_ids, a_ids, b_ids, nodes, nodes, nodes)
+        plan_and_gather_kernel,
+        out_shape=(table(count), table(4 * slots), table(4 * half), whole, whole, cut),
+        in_specs=[smem] * 5 + [pl.BlockSpec(memory_space=pltpu.HBM)],
+        out_specs=[smem] * 3 + [anywhere] * 3,
+        scratch_shapes=[
+            scratch(pair_nodes.shape[0]),
+            scratch(half),
+            scratch(count),
+            scratch(count),
+            scratch(count),
+            scratch(2 * half),
+            scratch(count),
+            pltpu.SemaphoreType.DMA,
+            pltpu.SemaphoreType.DMA,
+            pltpu.SemaphoreType.DMA,
+        ],
+        compiler_params=pltpu.CompilerParams(vmem_limit_bytes=48 * 2**20),
+    )(pair_nodes, prod_left, prod_right, prod_flag, prod_diag, nodes)
 
 
 def tile_product(left_re, left_im, right_re, right_im):
@@ -58,7 +176,8 @@
 def exchange_kernel(
     n,
     flags,
-    slots,
+    merges,
+    finals,
     left_send,
     a_send,
     b_send,
@@ -71,16 +190,22 @@
     right_pair,
     result,
     panels,
+    relayed,
+    merged,
     left_sem,
     a_sem,
     b_sem,
     swap_sem,
     result_sem,
+    relay_sem,
+    far_sem,
     left_out_sem,
     a_out_sem,
     b_out_sem,
     swap_out_sem,
     result_out_sem,
+    relay_out_sem,
+    far_out_sem,
 ):
     me = lax.axis_index("node")
     parity = lax.rem(me, 2)
@@ -160,6 +285,19 @@
         left_plain[0, down, across] = real_part
         left_plain[1, down, across] = imag_part
 
+    half = n // 2
+    slots = merged.shape[1]
+    near, far = pl.ds(0, half), pl.ds(half, slots)
+    side, place = lax.div(me, half), lax.rem(me, half)
+    mirror = lax.rem(me + half, n)
+
+    def rows_of(device):
+        return pl.ds(pl.multiple_of(device * rows, rows), rows)
+
+    for c in range(chunks):
+        panels[c][half + slots] = jnp.zeros(panels[c].shape[1:], panels[c].dtype)
+        relayed[c][half] = jnp.zeros(relayed[c].shape[1:], relayed[c].dtype)
+
     flipped = flags[me] == 1
 
     @pl.loop(0, tiles * tiles)
@@ -174,7 +312,7 @@
 
     landed(a_full, a_sem)
 
-    for c in range(chunks):
+    def compute(c):
         landed(b_full.at[c], b_sem.at[c])
 
         @pl.loop(0, tiles)
@@ -195,74 +333,88 @@
             result[c, 0, down, :] = real_part
             result[c, 1, down, :] = imag_part
 
-        @pl.loop(0, n - 1)
+        @pl.loop(1, half)
         def _(t):
-            to = target(t)
-            to_rows = pl.ds(pl.multiple_of(to * rows, rows), rows)
+            to = side * half + lax.rem(place + t, half)
             push(
-                result.at[c, :, to_rows],
-                panels[c].at[me],
+                result.at[c, :, rows_of(lax.rem(to + half, n))],
+                relayed[c].at[place],
+                relay_out_sem.at[c],
+                relay_sem.at[c],
+                to,
+            )
+
+        pltpu.make_async_copy(
+            result.at[c, :, rows_of(mirror)], relayed[c].at[place], relay_sem.at[c]
+        ).start()
+
+        @pl.loop(1, half)
+        def _(t):
+            to = side * half + lax.rem(place + t, half)
+            push(
+                result.at[c, :, rows_of(to)],
+                panels[c].at[place],
                 result_out_sem.at[c],
                 result_sem.at[c],
                 to,
             )
 
         pltpu.make_async_copy(
-            result.at[c, :, my_rows], panels[c].at[me], result_sem.at[c]
+            result.at[c, :, my_rows], panels[c].at[place], result_sem.at[c]
         ).start()
+
+    def merge(c):
+        landed(relayed[c].at[near], relay_sem.at[c])
+
+        @pl.loop(0, slots)
+        def _(t):
+            at = 2 * (side * slots + t)
+            first = relayed[c][merges[at]].astype(jnp.float32)
+            second = relayed[c][merges[at + 1]].astype(jnp.float32)
+            merged[c, t] = (first + second).astype(merged.dtype)
+
+        push(merged.at[c], panels[c].at[far], far_out_sem.at[c], far_sem.at[c], mirror)
+
+    for c in range(chunks):
+        compute(c)
+        if c > 0:
+            merge(c - 1)
+    merge(chunks - 1)
 
     width = b_full.shape[-1]
     for c in range(chunks):
-        landed(panels[c], result_sem.at[c])
+        landed(panels[c].at[near], result_sem.at[c])
+        landed(panels[c].at[far], far_sem.at[c])
 
         @pl.loop(0, out.shape[0])
         def _(d):
-            first = panels[c][slots[d, 0]].astype(jnp.float32)
-            second = panels[c][slots[d, 1]].astype(jnp.float32)
+            at = 2 * (side * out.shape[0] + d)
+            first = panels[c][finals[at]].astype(jnp.float32)
+            second = panels[c][finals[at + 1]].astype(jnp.float32)
             out[d, :, :, c * width : (c + 1) * width] = (first + second).astype(out.dtype)
 
     others = pl.ds(0, n - 1)
+    others_near = pl.ds(0, half - 1)
     landed(left_send.at[others], left_out_sem)
     landed(a_send.at[others], a_out_sem)
     landed(lefts.at[parity], swap_out_sem)
     for c in range(chunks):
         landed(b_send.at[c, others], b_out_sem.at[c])
-        landed(panels[c].at[others], result_out_sem.at[c])
+        landed(panels[c].at[others_near], result_out_sem.at[c])
+        landed(relayed[c].at[others_near], relay_out_sem.at[c])
+        landed(merged.at[c], far_out_sem.at[c])
 
 
 def local(nodes, pair_nodes, prod_left, prod_right, prod_flag, prod_diag, *, n):
     _, parts, rows, order = nodes.shape
     count = prod_left.shape[0]
     assert count == n and rows * n == order
-    diags = count // 2
+    half = diags = count // 2
+    slots = half // 2 + 1
     chunks = order // TILE
-    numbers = jnp.arange(count, dtype=jnp.int32)
-    ahead = (prod_left[None, :] < prod_left[:, None]) | (
-        (prod_left[None, :] == prod_left[:, None]) & (numbers[None, :] < numbers[:, None])
+    flags, merges, finals, left_send, a_send, b_send = plan_and_gather(
+        nodes, pair_nodes, prod_left, prod_right, prod_flag, prod_diag, chunks
     )
-    rank = jnp.sum(ahead.astype(jnp.int32), axis=1)
-    here = rank[None, :] == numbers[:, None]
-
-    def ordered(values):
-        return jnp.sum(jnp.where(here, values[None, :], 0), axis=1)
-
-    left_of, right_of = ordered(prod_left), ordered(prod_right)
-    flag_of, diag_of = ordered(prod_flag), ordered(prod_diag)
-
-    def node_of(pairs, side):
-        hot = pairs[:, None] == jnp.arange(pair_nodes.shape[0], dtype=jnp.int32)[None, :]
-        return jnp.sum(jnp.where(hot, side, 0), axis=1)
-
-    side = jnp.where(numbers[:, None] % 2 == 0, pair_nodes[None, :, 0], pair_nodes[None, :, 1])
-    left_ids = node_of(left_of, side)
-    a_ids = node_of(right_of, pair_nodes[None, :, 0])
-    b_ids = node_of(right_of, pair_nodes[None, :, 1])
-    mine = diag_of[None, :] == jnp.arange(diags, dtype=jnp.int32)[:, None]
-    first = jnp.min(jnp.where(mine, numbers[None, :], count), axis=1)
-    last = jnp.max(jnp.where(mine, numbers[None, :], -1), axis=1)
-    slots = jnp.stack([first, last], axis=1)
-
-    left_send, a_send, b_send = gather(nodes, left_ids, a_ids, b_ids, chunks)
     width = order // chunks
     kind = nodes.dtype
     dma = pltpu.SemaphoreType.DMA
@@ -271,7 +423,7 @@
     return pl.pallas_call(
         functools.partial(exchange_kernel, n),
         out_shape=jax.ShapeDtypeStruct((diags, parts, rows, order), kind),
-        in_specs=[smem, smem, anywhere, anywhere, anywhere],
+        in_specs=[smem, smem, smem, anywhere, anywhere, anywhere],
         out_specs=pl.BlockSpec(memory_space=pltpu.VMEM),
         scratch_shapes=[
             pltpu.VMEM((2, parts, order, order), kind),
@@ -281,22 +433,28 @@
             pltpu.VMEM((parts, order, order), kind),
             pltpu.VMEM((parts, order, width), kind),
             pltpu.VMEM((chunks, parts, order, width), kind),
-            [pltpu.VMEM((count, parts, rows, width), kind)] * chunks,
-            dma,
-            dma,
-            dma((chunks,)),
-            dma,
-            dma((chunks,)),
-            dma,
-            dma,
-            dma((chunks,)),
-            dma,
+            [pltpu.VMEM((half + slots + 1, parts, rows, width), kind)] * chunks,
+            [pltpu.VMEM((half + 1, parts, rows, width), kind)] * chunks,
+            pltpu.VMEM((chunks, slots, parts, rows, width), kind),
+            dma,
+            dma,
+            dma((chunks,)),
+            dma,
+            dma((chunks,)),
+            dma((chunks,)),
+            dma((chunks,)),
+            dma,
+            dma,
+            dma((chunks,)),
+            dma,
+            dma((chunks,)),
+            dma((chunks,)),
             dma((chunks,)),
         ],
         compiler_params=pltpu.CompilerParams(
-            collective_id=0, has_side_effects=True, vmem_limit_bytes=56 * 2**20
+            collective_id=0, has_side_effects=True, vmem_limit_bytes=40 * 2**20
         ),
-    )(flag_of, slots, left_send, a_send, b_send)
+    )(flags, merges, finals, left_send, a_send, b_send)
 
 
 def solution(mesh):

time: 390 us -> 600 us (1.54)
  Pallas kernels: 371 us -> 592 us
  local copies, waits for them, and re-layouts: 16.2 us -> 6.88 us
    pallas_call x1, Pallas kernels: 1.91 us -> 257 us  [plan_and_gather(): pl.pallas_call(plan_and_gather_kernel, out_shape=(table(count), table(4 *...]
    pallas_call x1, Pallas kernels: 369 us -> 335 us  [local(): pl.pallas_call(functools.partial(exchange_kernel, n), out_shape=jax.Shape...]
    unnamed x9 -> x12, local copies, waits for them, and re-layouts: 14.8 us -> 6.88 us
where the time goes in v2:
time: 600 us; the launch traced here: 599 us
  Pallas kernels  592 us (99%)
  local copies, waits for them, and re-layouts  6.88 us (1%)
    pallas_call x1, Pallas kernels, local(): pl.pallas_call(functools.partial(exchange_kernel, n), out_shape=jax.Shape...  335 us
    pallas_call x1, Pallas kernels, plan_and_gather(): pl.pallas_call(plan_and_gather_kernel, out_shape=(table(count), table(4 *...  257 us

profile of v2, /device:TPU:0, one launch (start us, length us, event | category | flops | bytes accessed | tf_op | source)
XLA Modules:
  0.0 599.4 jit_solution(12243691280856677597)
XLA Ops:
  0.0 0.8 copy.7.pair_nodes
  0.8 0.0 copy-start.1
  0.8 0.7 copy-done.1
  1.4 0.0 copy-start.2
  1.4 0.7 copy-done.2
  2.1 0.0 copy-start.3
  2.1 0.7 copy-done.3
  2.7 0.0 copy-start.4
  2.7 0.7 copy-done.4
  3.4 257.0 %shard_map.64 = (s32[16]{0:T(128)S(1)}, s32[20]{0:T(128)S(1)}, s32[32]{0:T(128)S(1)}, bf16[16,2,64,1024]{3,2,1,0:T(8,128)(2,1)S(1)}, bf16[16,2,64,1024]{3,2,1,0:...) custom-call(s32[16,2]{1,0:T(8,128)S(1)} %copy.7.pair_nodes, s32[16]{0:T(128)S(1)} %copy-done.1, s32[16]{0:T(128)S(1)} %copy-done.2, ...), custom_call_target="tpu_custom_call" | custom-call | tf_op jit(solution)/shard_map/pallas_call | solution.py:148
  260.4 0.0 copy-start
  260.4 2.2 copy-done
  262.6 335.5 %shard_map.65 = bf16[8,2,64,1024]{3,2,1,0:T(8,128)(2,1)S(1)} custom-call(s32[16]{0:T(128)S(1)} %get-tuple-element.11.flags, s32[20]{0:T(128)S(1)} %get-tuple-element.12.merges, s32[32]{0:T(128)S(1)} %get-tuple-element.13.finals, bf16[16,2,64,1024]{3,2,1,0:T(8,128)(2,1)S(1)} %get-tuple-element.14.left_send, bf16[16,2,64,1024]{3,2,1,0:T(8,128)(2,1)S(1)} %copy-done, ...), custom_call_target="tpu_custom_call" | custom-call | tf_op jit(solution)/shard_map/pallas_call | solution.py:423
  598.0 1.3 copy.9
Async XLA Ops:
  0.8 0.7 copy-start.1
  1.4 0.7 copy-start.2
  2.1 0.7 copy-start.3
  2.7 0.7 copy-start.4
  260.4 2.2 copy-start

commit v3 on v2

--- a/solution.py
+++ b/solution.py
@@ -143,13 +143,12 @@
     cut = jax.ShapeDtypeStruct((chunks, count, parts, rows, order // chunks), nodes.dtype)
     table = lambda size: jax.ShapeDtypeStruct((size,), jnp.int32)
     smem = pl.BlockSpec(memory_space=pltpu.SMEM)
-    anywhere = pl.BlockSpec(memory_space=pl.ANY)
     scratch = lambda size: pltpu.SMEM((size,), jnp.int32)
     return pl.pallas_call(
         plan_and_gather_kernel,
         out_shape=(table(count), table(4 * slots), table(4 * half), whole, whole, cut),
         in_specs=[smem] * 5 + [pl.BlockSpec(memory_space=pltpu.HBM)],
-        out_specs=[smem] * 3 + [anywhere] * 3,
+        out_specs=[smem] * 3 + [pl.BlockSpec(memory_space=pltpu.VMEM)] * 3,
         scratch_shapes=[
             scratch(pair_nodes.shape[0]),
             scratch(half),
@@ -162,7 +161,7 @@
             pltpu.SemaphoreType.DMA,
             pltpu.SemaphoreType.DMA,
         ],
-        compiler_params=pltpu.CompilerParams(vmem_limit_bytes=48 * 2**20),
+        compiler_params=pltpu.CompilerParams(vmem_limit_bytes=36 * 2**20),
     )(pair_nodes, prod_left, prod_right, prod_flag, prod_diag, nodes)
 
 
@@ -452,7 +451,7 @@
             dma((chunks,)),
         ],
         compiler_params=pltpu.CompilerParams(
-            collective_id=0, has_side_effects=True, vmem_limit_bytes=40 * 2**20
+            collective_id=0, has_side_effects=True, vmem_limit_bytes=38 * 2**20
         ),
     )(flags, merges, finals, left_send, a_send, b_send)
 

time: 600 us -> 347 us (0.58)
  Pallas kernels: 592 us -> 342 us
    pallas_call x1, Pallas kernels: 257 us -> 6.73 us  [plan_and_gather(): pl.pallas_call(plan_and_gather_kernel, out_shape=(table(count), table(4 *...]
where the time goes in v3:
time: 347 us
  Pallas kernels  342 us (99%)
  local copies, waits for them, and re-layouts  4.7 us (1%)
    pallas_call x1, Pallas kernels, local(): pl.pallas_call(functools.partial(exchange_kernel, n), out_shape=jax.Shape...  335 us

profile of v3, /device:TPU:0, one launch (start us, length us, event | category | flops | bytes accessed | tf_op | source)
XLA Modules:
  0.0 346.9 jit_solution(9612525353005601237)
XLA Ops:
  0.0 0.8 copy.7.pair_nodes
  0.8 0.0 copy-start
  0.8 0.7 copy-done
  1.4 0.0 copy-start.1
  1.4 0.7 copy-done.1
  2.1 0.0 copy-start.2
  2.1 0.7 copy-done.2
  2.7 0.0 copy-start.3
  2.7 0.7 copy-done.3
  3.4 6.7 %shard_map.64 = (s32[16]{0:T(128)S(1)}, s32[20]{0:T(128)S(1)}, s32[32]{0:T(128)S(1)}, bf16[16,2,64,1024]{3,2,1,0:T(8,128)(2,1)S(1)}, bf16[16,2,64,1024]{3,2,1,0:...) custom-call(s32[16,2]{1,0:T(8,128)S(1)} %copy.7.pair_nodes, s32[16]{0:T(128)S(1)} %copy-done, s32[16]{0:T(128)S(1)} %copy-done.1, ...), custom_call_target="tpu_custom_call" | custom-call | tf_op jit(solution)/shard_map/pallas_call | solution.py:147
  10.1 335.5 %shard_map.65 = bf16[8,2,64,1024]{3,2,1,0:T(8,128)(2,1)S(1)} custom-call(s32[16]{0:T(128)S(1)} %get-tuple-element.11.flags, s32[20]{0:T(128)S(1)} %get-tuple-element.12.merges, s32[32]{0:T(128)S(1)} %get-tuple-element.13.finals, bf16[16,2,64,1024]{3,2,1,0:T(8,128)(2,1)S(1)} %get-tuple-element.14.left_send, ...), custom_call_target="tpu_custom_call" | custom-call | tf_op jit(solution)/shard_map/pallas_call | solution.py:422
  345.6 1.3 copy.9
Async XLA Ops:
  0.8 0.7 copy-start
  1.4 0.7 copy-start.1
  2.1 0.7 copy-start.2
  2.7 0.7 copy-start.3

commit v4 on v3

--- a/solution.py
+++ b/solution.py
@@ -8,14 +8,11 @@
 from jax.sharding import PartitionSpec as P
 
 TILE = 256
+AHEAD = 2
 
 
 def plan_and_gather_kernel(
-    pair_nodes,
-    prod_left,
-    prod_right,
-    prod_flag,
-    prod_diag,
+    graph,
     nodes,
     flags,
     merges,
@@ -34,14 +31,15 @@
     a_sem,
     b_sem,
 ):
-    count = prod_left.shape[0]
+    count = graph.shape[1]
     diags = count // 2
     half = count // 2
+    first_node, prod_left, prod_right, prod_flag, prod_diag = 0, 2, 3, 4, 5
     slots = half // 2 + 1
     chunks = b_out.shape[0]
     width = b_out.shape[-1]
 
-    @pl.loop(0, pair_nodes.shape[0])
+    @pl.loop(0, count)
     def _(p):
         seen_left[p] = -1
 
@@ -55,8 +53,8 @@
     def _(k):
         done[k] = 0
         for group, seen, mate in (
-            (prod_left[k], seen_left, mate_left),
-            (prod_diag[k], seen_diag, mate_diag),
+            (graph[prod_left, k], seen_left, mate_left),
+            (graph[prod_diag, k], seen_diag, mate_diag),
         ):
             earlier = seen[group]
             found = earlier >= 0
@@ -71,15 +69,16 @@
         done[other] = 1
         order[2 * g] = now
         order[2 * g + 1] = other
-        for at, k in ((2 * g, now), (2 * g + 1, other)):
-            flags[at] = prod_flag[k]
-            left_id = pair_nodes[prod_left[k], at - 2 * g]
-            right = prod_right[k]
+        for side, k in ((first_node, now), (first_node + 1, other)):
+            at = 2 * g + side
+            flags[at] = graph[prod_flag, k]
+            left_id = graph[side, graph[prod_left, k]]
+            right = graph[prod_right, k]
             pltpu.make_async_copy(nodes.at[left_id], left_out.at[at], left_sem).start()
-            pltpu.make_async_copy(nodes.at[pair_nodes[right, 0]], a_out.at[at], a_sem).start()
+            pltpu.make_async_copy(nodes.at[graph[first_node, right]], a_out.at[at], a_sem).start()
             for c in range(chunks):
                 pltpu.make_async_copy(
-                    nodes.at[pair_nodes[right, 1], :, :, pl.ds(c * width, width)],
+                    nodes.at[graph[first_node + 1, right], :, :, pl.ds(c * width, width)],
                     b_out.at[c, at],
                     b_sem,
                 ).start()
@@ -88,6 +87,7 @@
             count,
             lambda k, best: jnp.where(done[count - 1 - k] == 0, count - 1 - k, best),
             jnp.int32(0),
+            unroll=True,
         )
         follow = mate_diag[other]
         return jnp.where(done[follow] == 0, follow, free)
@@ -103,7 +103,7 @@
             merges[2 * (base + t) + 1] = half
 
         def take(i, used):
-            diag = prod_diag[order[h * half + i]]
+            diag = graph[prod_diag, order[h * half + i]]
             slot = slot_of[h * diags + diag]
             new = slot < 0
             slot = jnp.where(new, used, slot)
@@ -140,6 +140,9 @@
     half = count // 2
     slots = half // 2 + 1
     whole = jax.ShapeDtypeStruct((count, parts, rows, order), nodes.dtype)
+    graph = jnp.stack(
+        [pair_nodes[:, 0], pair_nodes[:, 1], prod_left, prod_right, prod_flag, prod_diag]
+    )
     cut = jax.ShapeDtypeStruct((chunks, count, parts, rows, order // chunks), nodes.dtype)
     table = lambda size: jax.ShapeDtypeStruct((size,), jnp.int32)
     smem = pl.BlockSpec(memory_space=pltpu.SMEM)
@@ -147,10 +150,10 @@
     return pl.pallas_call(
         plan_and_gather_kernel,
         out_shape=(table(count), table(4 * slots), table(4 * half), whole, whole, cut),
-        in_specs=[smem] * 5 + [pl.BlockSpec(memory_space=pltpu.HBM)],
+        in_specs=[smem, pl.BlockSpec(memory_space=pltpu.HBM)],
         out_specs=[smem] * 3 + [pl.BlockSpec(memory_space=pltpu.VMEM)] * 3,
         scratch_shapes=[
-            scratch(pair_nodes.shape[0]),
+            scratch(count),
             scratch(half),
             scratch(count),
             scratch(count),
@@ -162,7 +165,7 @@
             pltpu.SemaphoreType.DMA,
         ],
         compiler_params=pltpu.CompilerParams(vmem_limit_bytes=36 * 2**20),
-    )(pair_nodes, prod_left, prod_right, prod_flag, prod_diag, nodes)
+    )(graph, nodes)
 
 
 def tile_product(left_re, left_im, right_re, right_im):
@@ -259,14 +262,16 @@
 
     pltpu.make_async_copy(a_send.at[me], a_full.at[:, my_rows], a_sem).start()
 
-    @pl.loop(0, chunks)
-    def _(c):
+    def push_right(c):
         @pl.loop(0, n - 1)
         def _(t):
             to = target(t)
             push(b_send.at[c, to], b_full.at[c, :, my_rows], b_out_sem.at[c], b_sem.at[c], to)
 
         pltpu.make_async_copy(b_send.at[c, me], b_full.at[c, :, my_rows], b_sem.at[c]).start()
+
+    for c in range(min(AHEAD, chunks)):
+        push_right(c)
 
     landed(lefts.at[parity], left_sem)
     push(lefts.at[parity], lefts.at[parity], swap_out_sem, swap_sem, partner)
@@ -376,6 +381,8 @@
 
     for c in range(chunks):
         compute(c)
+        if c + AHEAD < chunks:
+            push_right(c + AHEAD)
         if c > 0:
             merge(c - 1)
     merge(chunks - 1)
@@ -407,7 +414,7 @@
 def local(nodes, pair_nodes, prod_left, prod_right, prod_flag, prod_diag, *, n):
     _, parts, rows, order = nodes.shape
     count = prod_left.shape[0]
-    assert count == n and rows * n == order
+    assert count == n == pair_nodes.shape[0] and rows * n == order
     half = diags = count // 2
     slots = half // 2 + 1
     chunks = order // TILE

time: 347 us -> 346 us (level)
  no operation moved by 1% of the time
where the time goes in v4:
time: 346 us; the launch traced here: 343 us
  Pallas kernels  340 us (98%)
    pallas_call x1, Pallas kernels, local(): pl.pallas_call(functools.partial(exchange_kernel, n), out_shape=jax.Shape...  334 us

profile of v4, /device:TPU:0, one launch (start us, length us, event | category | flops | bytes accessed | tf_op | source)
XLA Modules:
  0.0 343.2 jit_solution(15753709811650295478)
XLA Ops:
  0.0 0.8 slice_bitcast_fusion
  0.8 0.7 stack.19.graph
  1.5 6.7 %shard_map.64 = (s32[16]{0:T(128)S(1)}, s32[20]{0:T(128)S(1)}, s32[32]{0:T(128)S(1)}, bf16[16,2,64,1024]{3,2,1,0:T(8,128)(2,1)S(1)}, bf16[16,2,64,1024]{3,2,1,0:...) custom-call(s32[6,16]{1,0:T(8,128)S(1)} %stack.19.graph, bf16[64,2,64,1024]{3,2,1,0:T(8,128)(2,1)} %nodes.1), custom_call_target="tpu_custom_call" | custom-call | tf_op jit(solution)/shard_map/pallas_call | solution.py:150
  8.2 333.7 %shard_map.65 = bf16[8,2,64,1024]{3,2,1,0:T(8,128)(2,1)S(1)} custom-call(s32[16]{0:T(128)S(1)} %get-tuple-element.11.flags, s32[20]{0:T(128)S(1)} %get-tuple-element.12.merges, s32[32]{0:T(128)S(1)} %get-tuple-element.13.finals, bf16[16,2,64,1024]{3,2,1,0:T(8,128)(2,1)S(1)} %get-tuple-element.14.left_send, ...), custom_call_target="tpu_custom_call" | custom-call | tf_op jit(solution)/shard_map/pallas_call | solution.py:429
  341.9 1.3 copy.8

commit v5 on v4

--- a/solution.py
+++ b/solution.py
@@ -36,8 +36,6 @@
     half = count // 2
     first_node, prod_left, prod_right, prod_flag, prod_diag = 0, 2, 3, 4, 5
     slots = half // 2 + 1
-    chunks = b_out.shape[0]
-    width = b_out.shape[-1]
 
     @pl.loop(0, count)
     def _(p):
@@ -76,12 +74,9 @@
             right = graph[prod_right, k]
             pltpu.make_async_copy(nodes.at[left_id], left_out.at[at], left_sem).start()
             pltpu.make_async_copy(nodes.at[graph[first_node, right]], a_out.at[at], a_sem).start()
-            for c in range(chunks):
-                pltpu.make_async_copy(
-                    nodes.at[graph[first_node + 1, right], :, :, pl.ds(c * width, width)],
-                    b_out.at[c, at],
-                    b_sem,
-                ).start()
+            pltpu.make_async_copy(
+                nodes.at[graph[first_node + 1, right]], b_out.at[at], b_sem
+            ).start()
         free = lax.fori_loop(
             0,
             count,
@@ -134,7 +129,7 @@
     pltpu.make_async_copy(b_out, b_out, b_sem).wait()
 
 
-def plan_and_gather(nodes, pair_nodes, prod_left, prod_right, prod_flag, prod_diag, chunks):
+def plan_and_gather(nodes, pair_nodes, prod_left, prod_right, prod_flag, prod_diag):
     count = prod_left.shape[0]
     _, parts, rows, order = nodes.shape
     half = count // 2
@@ -143,13 +138,12 @@
     graph = jnp.stack(
         [pair_nodes[:, 0], pair_nodes[:, 1], prod_left, prod_right, prod_flag, prod_diag]
     )
-    cut = jax.ShapeDtypeStruct((chunks, count, parts, rows, order // chunks), nodes.dtype)
     table = lambda size: jax.ShapeDtypeStruct((size,), jnp.int32)
     smem = pl.BlockSpec(memory_space=pltpu.SMEM)
     scratch = lambda size: pltpu.SMEM((size,), jnp.int32)
     return pl.pallas_call(
         plan_and_gather_kernel,
-        out_shape=(table(count), table(4 * slots), table(4 * half), whole, whole, cut),
+        out_shape=(table(count), table(4 * slots), table(4 * half), whole, whole, whole),
         in_specs=[smem, pl.BlockSpec(memory_space=pltpu.HBM)],
         out_specs=[smem] * 3 + [pl.BlockSpec(memory_space=pltpu.VMEM)] * 3,
         scratch_shapes=[
@@ -263,12 +257,16 @@
     pltpu.make_async_copy(a_send.at[me], a_full.at[:, my_rows], a_sem).start()
 
     def push_right(c):
+        columns = pl.ds(c * b_full.shape[-1], b_full.shape[-1])
+
         @pl.loop(0, n - 1)
         def _(t):
             to = target(t)
-            push(b_send.at[c, to], b_full.at[c, :, my_rows], b_out_sem.at[c], b_sem.at[c], to)
-
-        pltpu.make_async_copy(b_send.at[c, me], b_full.at[c, :, my_rows], b_sem.at[c]).start()
+            push(b_send.at[to, :, :, columns], b_full.at[c, :, my_rows], b_out_sem.at[c], b_sem.at[c], to)
+
+        pltpu.make_async_copy(
+            b_send.at[me, :, :, columns], b_full.at[c, :, my_rows], b_sem.at[c]
+        ).start()
 
     for c in range(min(AHEAD, chunks)):
         push_right(c)
@@ -399,13 +397,13 @@
             second = panels[c][finals[at + 1]].astype(jnp.float32)
             out[d, :, :, c * width : (c + 1) * width] = (first + second).astype(out.dtype)
 
-    others = pl.ds(0, n - 1)
+    others, sent_rows = pl.ds(0, n - 1), pl.ds(0, (n - 1) * rows)
     others_near = pl.ds(0, half - 1)
     landed(left_send.at[others], left_out_sem)
     landed(a_send.at[others], a_out_sem)
     landed(lefts.at[parity], swap_out_sem)
     for c in range(chunks):
-        landed(b_send.at[c, others], b_out_sem.at[c])
+        landed(b_full.at[c, :, sent_rows], b_out_sem.at[c])
         landed(panels[c].at[others_near], result_out_sem.at[c])
         landed(relayed[c].at[others_near], relay_out_sem.at[c])
         landed(merged.at[c], far_out_sem.at[c])
@@ -419,7 +417,7 @@
     slots = half // 2 + 1
     chunks = order // TILE
     flags, merges, finals, left_send, a_send, b_send = plan_and_gather(
-        nodes, pair_nodes, prod_left, prod_right, prod_flag, prod_diag, chunks
+        nodes, pair_nodes, prod_left, prod_right, prod_flag, prod_diag
     )
     width = order // chunks
     kind = nodes.dtype

time: 346 us -> 346 us (level)
  no operation moved by 1% of the time
where the time goes in v5:
time: 346 us; the launch traced here: 343 us
  Pallas kernels  340 us (98%)
    pallas_call x1, Pallas kernels, local(): pl.pallas_call(functools.partial(exchange_kernel, n), out_shape=jax.Shape...  334 us

profile of v5, /device:TPU:0, one launch (start us, length us, event | category | flops | bytes accessed | tf_op | source)
XLA Modules:
  0.0 343.0 jit_solution(18110748096887731418)
XLA Ops:
  0.0 0.8 slice_bitcast_fusion
  0.8 0.7 stack.19.graph
  1.5 6.5 %shard_map.64 = (s32[16]{0:T(128)S(1)}, s32[20]{0:T(128)S(1)}, s32[32]{0:T(128)S(1)}, bf16[16,2,64,1024]{3,2,1,0:T(8,128)(2,1)S(1)}, bf16[16,2,64,1024]{3,2,1,0:...) custom-call(s32[6,16]{1,0:T(8,128)S(1)} %stack.19.graph, bf16[64,2,64,1024]{3,2,1,0:T(8,128)(2,1)} %nodes.1), custom_call_target="tpu_custom_call" | custom-call | tf_op jit(solution)/shard_map/pallas_call | solution.py:144
  8.0 333.7 %shard_map.65 = bf16[8,2,64,1024]{3,2,1,0:T(8,128)(2,1)S(1)} custom-call(s32[16]{0:T(128)S(1)} %get-tuple-element.11.flags, s32[20]{0:T(128)S(1)} %get-tuple-element.12.merges, s32[32]{0:T(128)S(1)} %get-tuple-element.13.finals, bf16[16,2,64,1024]{3,2,1,0:T(8,128)(2,1)S(1)} %get-tuple-element.14.left_send, ...), custom_call_target="tpu_custom_call" | custom-call | tf_op jit(solution)/shard_map/pallas_call | solution.py:427
  341.7 1.3 copy.8

commit v6 on v4

--- a/solution.py
+++ b/solution.py
@@ -8,7 +8,8 @@
 from jax.sharding import PartitionSpec as P
 
 TILE = 256
-AHEAD = 2
+AHEAD = 4
+WIDTH = 128
 
 
 def plan_and_gather_kernel(
@@ -417,7 +418,7 @@
     assert count == n == pair_nodes.shape[0] and rows * n == order
     half = diags = count // 2
     slots = half // 2 + 1
-    chunks = order // TILE
+    chunks = order // WIDTH
     flags, merges, finals, left_send, a_send, b_send = plan_and_gather(
         nodes, pair_nodes, prod_left, prod_right, prod_flag, prod_diag, chunks
     )

time: 346 us -> 346 us (level)
  no operation moved by 1% of the time
where the time goes in v6:
time: 346 us; the launch traced here: 345 us
  Pallas kernels  342 us (99%)
    pallas_call x1, Pallas kernels, local(): pl.pallas_call(functools.partial(exchange_kernel, n), out_shape=jax.Shape...  335 us

profile of v6, /device:TPU:0, one launch (start us, length us, event | category | flops | bytes accessed | tf_op | source)
XLA Modules:
  0.0 344.7 jit_solution(11707573348124500910)
XLA Ops:
  0.0 0.8 slice_bitcast_fusion
  0.8 0.7 stack.19.graph
  1.5 6.8 %shard_map.64 = (s32[16]{0:T(128)S(1)}, s32[20]{0:T(128)S(1)}, s32[32]{0:T(128)S(1)}, bf16[16,2,64,1024]{3,2,1,0:T(8,128)(2,1)S(1)}, bf16[16,2,64,1024]{3,2,1,0:...) custom-call(s32[6,16]{1,0:T(8,128)S(1)} %stack.19.graph, bf16[64,2,64,1024]{3,2,1,0:T(8,128)(2,1)} %nodes.1), custom_call_target="tpu_custom_call" | custom-call | tf_op jit(solution)/shard_map/pallas_call | solution.py:151
  8.2 335.1 %shard_map.65 = bf16[8,2,64,1024]{3,2,1,0:T(8,128)(2,1)S(1)} custom-call(s32[16]{0:T(128)S(1)} %get-tuple-element.11.flags, s32[20]{0:T(128)S(1)} %get-tuple-element.12.merges, s32[32]{0:T(128)S(1)} %get-tuple-element.13.finals, bf16[16,2,64,1024]{3,2,1,0:T(8,128)(2,1)S(1)} %get-tuple-element.14.left_send, ...), custom_call_target="tpu_custom_call" | custom-call | tf_op jit(solution)/shard_map/pallas_call | solution.py:430
  343.4 1.3 copy.8
